TPU v7x, 32 devices: a whole 2x2x4 slice. The times are simulated.
32 devices in a mesh: groups: 2 (over y), view: 4 (over z), row: 4 (over x, core).
Axes of the slice: x: 2, y: 2, z: 4, core: 2. Of those that a mesh axis runs over, the one named last changes fastest.
Arguments:
- inputs: bfloat16 [64, 292, 16, 16], P(None, 'view', ('groups', 'row')), parts along dimension 2, may hold values from -24 to 24
- cotangent: bfloat16 [64, 292, 16, 16], P(None, None, ('groups', 'row'), 'view'), parts along dimension 2, may hold values from -6 to 6
- keep: int32 [584], P('groups'), parts along dimension 0, may hold values from 0 to 1, as said below
- w_conv: bfloat16 [64, 64, 3, 3], replicated, may hold values from -0.25 to 0.25
- gain: float32 [64], replicated, may hold values from 0.5 to 1.5
- w_query: bfloat16 [64, 64], replicated, may hold values from -3 to 3
- w_key: bfloat16 [64, 64], replicated, may hold values from -3 to 3
- w_value: bfloat16 [64, 64], replicated, may hold values from -0.75 to 0.75
- w_out: bfloat16 [64, 64], replicated, may hold values from -0.75 to 0.75
Outputs:
- output: bfloat16 [64, 292, 16, 16], P(None, None, ('groups', 'row'), 'view'), parts along dimension 2
- d_input: bfloat16 [64, 292, 16, 16], P(None, 'view', ('groups', 'row')), parts along dimension 2
- g_conv: float32 [128, 64, 3, 3], P('groups'), parts along dimension 0
- g_gain: float32 [128], P('groups'), parts along dimension 0
- g_query: float32 [128, 64], P('groups'), parts along dimension 0
- g_key: float32 [128, 64], P('groups'), parts along dimension 0
- g_value: float32 [128, 64], P('groups'), parts along dimension 0
- g_out: float32 [128, 64], P('groups'), parts along dimension 0
There are 2 independent parts, one for each index of `groups`. A program takes and returns all parts, laid end to end along the dimension named above; an argument that names none is the same for every part. Nothing has to cross between parts.
Inputs may be any that keep to these rules, and one draw needn't show every extreme that they name: `keep`: zero at every view from 289 on, one at view 289 // 2.
All inputs are finite; a program needn't handle non-finite values.
Results may differ from a plain program's by a relative error of at most 0.012.
The roundings to bfloat16 on the way count: a program that leaves them out, or rounds other values in their place, can miss the bound.
Values may be sent and summed in bfloat16 or wider, within the bound.
No kernel may reach another device: no remote copies, remote signals or barrier semaphores. Data moves between devices by JAX's collectives and lax.ppermute only.
A program may use at most 64 MiB of HBM per device.

v0:
```python
import math
import jax
import jax.numpy as jnp
from jax import lax
from jax.sharding import PartitionSpec as P


def with_halo(cells, sides, width):
    for axis, dim in sides:
        count = lax.axis_size(axis)
        ends = count - 1
        head = lax.slice_in_dim(cells, 0, width, axis=dim)
        tail = lax.slice_in_dim(cells, cells.shape[dim] - width, cells.shape[dim], axis=dim)
        cells = jnp.concatenate(
            [
                lax.ppermute(tail, axis, [(i, (i + 1) % count) for i in range(ends)]),
                cells,
                lax.ppermute(head, axis, [((i + 1) % count, i) for i in range(ends)]),
            ],
            axis=dim,
        )
    return cells


def product(form, left, right):
    return jnp.einsum(form, left, right, preferred_element_type=jnp.float32)


def convolve(padded, w_conv):
    height = padded.shape[2] - 2
    breadth = padded.shape[3] - 2
    total = jnp.zeros((w_conv.shape[0], padded.shape[1], height, breadth), jnp.float32)
    for row_tap in range(3):
        for col_tap in range(3):
            window = padded[:, :, row_tap : row_tap + height, col_tap : col_tap + breadth]
            total = total + product("oc,cvrw->ovrw", w_conv[:, :, row_tap, col_tap], window)
    return total


def input_grad(grad_pad, w_conv):
    height = grad_pad.shape[2] - 2
    breadth = grad_pad.shape[3] - 2
    total = jnp.zeros((w_conv.shape[1], grad_pad.shape[1], height, breadth), jnp.float32)
    for row_tap in range(3):
        for col_tap in range(3):
            window = grad_pad[
                :, :, 2 - row_tap : 2 - row_tap + height, 2 - col_tap : 2 - col_tap + breadth
            ]
            total = total + product("oc,ovrw->cvrw", w_conv[:, :, row_tap, col_tap], window)
    return total


def weight_grad(grad, padded):
    height = grad.shape[2]
    breadth = grad.shape[3]
    taps = []
    for row_tap in range(3):
        for col_tap in range(3):
            window = padded[:, :, row_tap : row_tap + height, col_tap : col_tap + breadth]
            taps.append(product("ovrw,cvrw->oc", grad, window))
    stacked = jnp.stack(taps, axis=2)
    return stacked.reshape(grad.shape[0], padded.shape[0], 3, 3)


def angular(mixed_in, grad_out, keep, gain, w_query, w_key, w_value, w_out, used):
    pixels, all_views, channels = mixed_in.shape
    scale = 1.0 / math.sqrt(channels)
    values = mixed_in.astype(jnp.float32)
    centred = values - jnp.mean(values, axis=2, keepdims=True)
    rstd = lax.rsqrt(jnp.mean(centred * centred, axis=2, keepdims=True) + 1e-05)
    normed = centred * rstd
    normal_in = (normed * gain[None, None, :]).astype(jnp.bfloat16)
    query = product("cd,pvc->pvd", w_query, normal_in).astype(jnp.bfloat16)
    key_proj = product("cd,pvc->pvd", w_key, normal_in).astype(jnp.bfloat16)
    value_proj = product("cd,pvc->pvd", w_value, normal_in).astype(jnp.bfloat16)
    scores = product("pvd,pud->pvu", query, key_proj) * scale
    scores = jnp.where(keep[None, None, :used] > 0, scores, -1e30)
    highest = jnp.max(scores, axis=2, keepdims=True)
    expo = jnp.exp(scores - highest)
    probs = expo / jnp.sum(expo, axis=2, keepdims=True)
    probs_b = probs.astype(jnp.bfloat16)
    attended = product("pvu,pud->pvd", probs_b, value_proj).astype(jnp.bfloat16)
    output = (values + product("dc,pvd->pvc", w_out, attended)).astype(jnp.bfloat16)
    d_attended = product("dc,pvc->pvd", w_out, grad_out).astype(jnp.bfloat16)
    g_out = product("pvd,pvc->dc", attended, grad_out)
    d_probs = product("pvd,pud->pvu", d_attended, value_proj)
    d_value = product("pvu,pvd->pud", probs_b, d_attended).astype(jnp.bfloat16)
    inner = jnp.sum(probs * d_probs, axis=2, keepdims=True)
    d_scores = (probs * (d_probs - inner) * scale).astype(jnp.bfloat16)
    d_query = product("pvu,pud->pvd", d_scores, key_proj).astype(jnp.bfloat16)
    d_key = product("pvu,pvd->pud", d_scores, query).astype(jnp.bfloat16)
    g_query = product("pvc,pvd->cd", normal_in, d_query)
    g_key = product("pvc,pvd->cd", normal_in, d_key)
    g_value = product("pvc,pvd->cd", normal_in, d_value)
    d_normal = (
        product("cd,pvd->pvc", w_query, d_query)
        + product("cd,pvd->pvc", w_key, d_key)
        + product("cd,pvd->pvc", w_value, d_value)
    )
    g_gain = jnp.sum(d_normal * normed, axis=(0, 1))
    scaled = d_normal * gain[None, None, :]
    back = (
        scaled
        - jnp.mean(scaled, axis=2, keepdims=True)
        - normed * jnp.mean(scaled * normed, axis=2, keepdims=True)
    )
    d_spatial = (grad_out.astype(jnp.float32) + back * rstd).astype(jnp.bfloat16)
    return (output, d_spatial, (g_gain, g_query, g_key, g_value, g_out))


def angular_rows(spatial, cotangent, keep, gain, w_query, w_key, w_value, w_out, used):

    def row_pass(pair):
        return angular(pair[0], pair[1], keep, gain, w_query, w_key, w_value, w_out, used)

    spatial_last = jnp.transpose(spatial, (2, 3, 1, 0))
    cotangent_last = jnp.transpose(cotangent, (2, 3, 1, 0))
    out_rows, grad_rows, grads = lax.map(row_pass, (spatial_last, cotangent_last))
    summed = tuple((jnp.sum(item, axis=0) for item in grads))
    return (jnp.transpose(out_rows, (3, 2, 0, 1)), jnp.transpose(grad_rows, (3, 2, 0, 1)), summed)


def body(inputs, cotangent, keep, w_conv, gain, w_query, w_key, w_value, w_out):
    channels, view_dev, row_dev, width = inputs.shape
    blocks = lax.axis_size("view")
    breadth = width // blocks
    all_views = view_dev * blocks
    padded = with_halo(inputs, (("row", 2),), 1)
    padded = jnp.pad(padded, ((0, 0), (0, 0), (0, 0), (1, 1)))
    spatial = (inputs.astype(jnp.float32) + convolve(padded, w_conv)).astype(jnp.bfloat16)
    moved = lax.all_to_all(
        spatial.reshape(channels, view_dev, row_dev, blocks, breadth),
        "view",
        split_axis=3,
        concat_axis=1,
        tiled=True,
    )
    moved = moved.reshape(channels, all_views, row_dev, breadth)
    output, d_spatial, grads = angular_rows(
        moved, cotangent, keep, gain, w_query, w_key, w_value, w_out, all_views
    )
    returned = lax.all_to_all(
        d_spatial.reshape(channels, all_views, row_dev, 1, breadth),
        "view",
        split_axis=1,
        concat_axis=3,
        tiled=True,
    )
    returned = returned.reshape(channels, view_dev, row_dev, width)
    grad_pad = with_halo(returned, (("row", 2),), 1)
    grad_pad = jnp.pad(grad_pad, ((0, 0), (0, 0), (0, 0), (1, 1)))
    d_input = (returned.astype(jnp.float32) + input_grad(grad_pad, w_conv)).astype(jnp.bfloat16)
    g_conv = weight_grad(returned, padded)
    g_gain, g_query, g_key, g_value, g_out = grads
    g_conv, g_gain, g_query, g_key, g_value, g_out = lax.psum(
        (g_conv, g_gain, g_query, g_key, g_value, g_out), ("view", "row")
    )
    return (output, d_input, g_conv, g_gain, g_query, g_key, g_value, g_out)


def solution(mesh):
    placed = (
        P(None, "view", ("groups", "row"), None),
        P(None, None, ("groups", "row"), "view"),
        P("groups"),
        P(),
        P(),
        P(),
        P(),
        P(),
        P(),
    )
    return jax.shard_map(
        body,
        mesh=mesh,
        in_specs=placed,
        out_specs=(
            P(None, None, ("groups", "row"), "view"),
            P(None, "view", ("groups", "row"), None),
            P("groups", None, None, None),
            P("groups"),
            P("groups", None),
            P("groups", None),
            P("groups", None),
            P("groups", None),
        ),
        check_vma=False,
    )
```

profile of v0, /device:TPU:0, one launch (start us, length us, event | category | flops | bytes accessed | tf_op | source)
XLA Modules:
  0.0 311.2 jit_solution(1073874773569292355)
XLA Ops:
  8.4 2.4 collective-permute-start
  10.9 1.3 collective-permute-start.1
  13.2 3.2 %collective-permute-done.1 = bf16[64,73,1,16]{1,0,3,2:T(8,128)(2,1)S(1)} collective-permute-done((bf16[64,73,1,16]{1,0,3,2:T(8,128)(2,1)S(1)}, bf16[64,73,1,16]{1,0,3,2:T(8,128)(2,1)S(1)}, u32[]{:S(2)}, u32[]{:S(2)}) %collective-permute-start.1) | collective-permute-done | bytes 149536 | tf_op jit(solution)/shard_map/ppermute | solution.py:18
  20.0 5.0 %all-to-all-start = ((bf16[64,73,2,4,4]{1,0,4,2,3:T(8,128)(2,1)}), bf16[64,73,2,4,4]{1,0,4,2,3:T(8,128)(2,1)S(1)}, u32[]{:S(2)}, u32[]{:S(2)}) async-start(bf16[64,73,2,4,4]{1,0,4,2,3:T(8,128)(2,1)} %copy.93), calls=%async_computation | async-start | bytes 1048576 | tf_op jit(solution)/shard_map/all_to_all | solution.py:131
  25.1 12.3 %all-to-all-done = bf16[64,73,2,4,4]{1,0,4,2,3:T(8,128)(2,1)S(1)} async-done(((bf16[64,73,2,4,4]{1,0,4,2,3:T(8,128)(2,1)}), bf16[64,73,2,4,4]{1,0,4,2,3:T(8,128)(2,1)S(1)}, u32[]{:S(2)}, u32[]{:S(2)}) %all-to-all-start) | async-done | bytes 299040 | tf_op jit(solution)/shard_map/all_to_all | solution.py:131
  38.2 56.6 %while.22 = (s32[]{:T(128)}, bf16[2,4,292,64]{2,1,0,3:T(4,128)(2,1)}, bf16[2,4,292,64]{2,3,1,0:T(8,128)(2,1)}, f32[2,64]{1,0:T(2,128)}, f32[2,64,64]{2,1,0:T(8,1...) while((s32[]{:T(128)}, ...), condition=%wide.region_9.10_spmd, body=%wide.region_0.9_spmd.sunk | while | flops 399432576 | bytes 35407752 | solution.py:118
  39.8 1.5 fusion.290
  41.3 1.6 convolution_convert_fusion.12
  42.9 3.1 %fusion.288 = (f32[4,292]{1,0:T(4,128)S(1)}, f32[4,292,292]{1,2,0:T(8,128)}) fusion(pred[292]{0:T(512)(128)(4,1)S(1)} %broadcast_compare_fusion.2, bf16[4,292,64]{1,2,0:T(8,128)(2,1)} %convolution_convert_fusion.12, bf16[64,64]{1,0:T(8,128)(2,1)S(1)} %copy-done.17, f32[64]{0:T(128)} %get-tuple-element.425, f32[4,292]{1,0:T(4,128)S(1)} %add_rsqrt_fusion.2, ...), kind=kOutput, calls=%fused_computation.193.clone.1 | convolution fusion | flops 55036452 | bytes 1744452 | tf_op jit(solution)/shard_map/while/body/eval_jaxpr/sub | solution.py:79
  46.0 3.5 %fusion.293 = bf16[4,292,64]{1,2,0:T(8,128)(2,1)} fusion(f32[4,292,292]{1,2,0:T(8,128)S(1)} %fusion.290, f32[4,292,292]{1,2,0:T(8,128)} %get-tuple-element.288, f32[4,292]{1,0:T(4,128)S(1)} %get-tuple-element.289, bf16[64,64]{1,0:T(8,128)(2,1)S(1)} %copy-done.17, f32[64]{0:T(128)} %get-tuple-element.425, f32[4,292]{1,0:T(4,128)S(1)} %add_rsqrt_fusion.2, ...), kind=kOutput, calls=%fused_computation.14.clone.1 | convolution fusion | flops 56135540 | bytes 7662592 | tf_op jit(solution)/shard_map/while/body/eval_jaxpr/pvu,pvd->pud/dot_general | solution.py:26
  49.6 3.5 %fusion.291 = bf16[4,292,64]{1,2,0:T(8,128)(2,1)} fusion(bf16[4,292,64]{1,2,0:T(8,128)(2,1)} %convolution_convert_fusion.12, f32[4,292,292]{1,2,0:T(8,128)S(1)} %fusion.290, f32[4,292,292]{1,2,0:T(8,128)} %get-tuple-element.288, f32[4,292]{1,0:T(4,128)S(1)} %get-tuple-element.289), kind=kOutput, calls=%fused_computation.13.clone.1 | convolution fusion | flops 46118772 | bytes 3032128 | tf_op jit(solution)/shard_map/while/body/eval_jaxpr/pvu,pud->pvd/dot_general | solution.py:26
  55.3 2.0 convolution_convert_fusion.15
  62.5 1.9 convolution_convert_fusion.13
  68.1 1.5 fusion.290
  69.6 1.6 convolution_convert_fusion.12
  71.2 3.1 %fusion.288 = (f32[4,292]{1,0:T(4,128)S(1)}, f32[4,292,292]{1,2,0:T(8,128)}) fusion(pred[292]{0:T(512)(128)(4,1)S(1)} %broadcast_compare_fusion.2, bf16[4,292,64]{1,2,0:T(8,128)(2,1)} %convolution_convert_fusion.12, bf16[64,64]{1,0:T(8,128)(2,1)S(1)} %copy-done.17, f32[64]{0:T(128)} %get-tuple-element.425, f32[4,292]{1,0:T(4,128)S(1)} %add_rsqrt_fusion.2, ...), kind=kOutput, calls=%fused_computation.193.clone.1 | convolution fusion | flops 55036452 | bytes 1744452 | tf_op jit(solution)/shard_map/while/body/eval_jaxpr/sub | solution.py:79
  74.3 3.5 %fusion.293 = bf16[4,292,64]{1,2,0:T(8,128)(2,1)} fusion(f32[4,292,292]{1,2,0:T(8,128)S(1)} %fusion.290, f32[4,292,292]{1,2,0:T(8,128)} %get-tuple-element.288, f32[4,292]{1,0:T(4,128)S(1)} %get-tuple-element.289, bf16[64,64]{1,0:T(8,128)(2,1)S(1)} %copy-done.17, f32[64]{0:T(128)} %get-tuple-element.425, f32[4,292]{1,0:T(4,128)S(1)} %add_rsqrt_fusion.2, ...), kind=kOutput, calls=%fused_computation.14.clone.1 | convolution fusion | flops 56135540 | bytes 7662592 | tf_op jit(solution)/shard_map/while/body/eval_jaxpr/pvu,pvd->pud/dot_general | solution.py:26
  77.9 3.5 %fusion.291 = bf16[4,292,64]{1,2,0:T(8,128)(2,1)} fusion(bf16[4,292,64]{1,2,0:T(8,128)(2,1)} %convolution_convert_fusion.12, f32[4,292,292]{1,2,0:T(8,128)S(1)} %fusion.290, f32[4,292,292]{1,2,0:T(8,128)} %get-tuple-element.288, f32[4,292]{1,0:T(4,128)S(1)} %get-tuple-element.289), kind=kOutput, calls=%fused_computation.13.clone.1 | convolution fusion | flops 46118772 | bytes 3032128 | tf_op jit(solution)/shard_map/while/body/eval_jaxpr/pvu,pud->pvd/dot_general | solution.py:26
  83.6 2.0 convolution_convert_fusion.15
  90.8 1.9 convolution_convert_fusion.13
  94.8 1.6 copy.97
  97.8 5.2 %all-to-all-start.1 = ((bf16[4,2,18688]{2,1,0:T(2,128)(2,1)}), bf16[4,2,18688]{2,1,0:T(2,128)(2,1)S(1)}, u32[]{:S(2)}, u32[]{:S(2)}) async-start(bf16[4,2,18688]{2,1,0:T(2,128)(2,1)} %reshape.106), calls=%async_computation.1 | async-start | bytes 598016 | tf_op jit(solution)/shard_map/all_to_all | solution.py:142
  106.3 6.2 %all-to-all-done.1 = bf16[4,2,18688]{2,1,0:T(2,128)(2,1)S(1)} async-done(((bf16[4,2,18688]{2,1,0:T(2,128)(2,1)}), bf16[4,2,18688]{2,1,0:T(2,128)(2,1)S(1)}, u32[]{:S(2)}, u32[]{:S(2)}) %all-to-all-start.1) | async-done | bytes 299040 | tf_op jit(solution)/shard_map/all_to_all | solution.py:142
  117.4 1.3 collective-permute-start.3
  118.7 4.0 %collective-permute-start.2 = (bf16[64,73,1,16]{1,0,3,2:T(8,128)(2,1)S(1)}, bf16[64,73,1,16]{1,0,3,2:T(8,128)(2,1)S(1)}, u32[]{:S(2)}, u32[]{:S(2)}) collective-permute-start(bf16[64,73,1,16]{1,0,3,2:T(8,128)(2,1)S(1)} %get-tuple-element.172), channel_id=1, source_target_pairs={{0,1},{1,2},{2,3},{4,5},{5,6},{6,7},{8,9},{9,10},{10,11},{12,13},{... | collective-permute-start | bytes 448520 | tf_op jit(solution)/shard_map/ppermute | solution.py:16
  127.6 71.4 %all-reduce.8.cloned.1.call-done = (f32[64]{0:T(128)}, f32[64,64]{1,0:T(8,128)}, f32[64,64]{1,0:T(8,128)}, f32[64,64]{1,0:T(8,128)}, f32[64,64]{1,0:T(8,128)}) async-done(((f32[64]{0:T(128)}, f32[64,64]{1,0:T(8,128)}, f32[64,64]{1,0:T(8,128)}, f32[64,64]{1,0:T(8,128)}, f32[64,64]{1,0:T(8,128)}), (f32[64]{0:T(128)}, f32[64,64]{1,0:T(8,128)}, f32[64,64]{1,0:T(8,128)}, f32[64,64]{1,0:T(8,128)}, ...) | async-done | bytes 65808 | tf_op jit(solution)/shard_map/psum | solution.py:155
  199.0 97.0 %all-reduce.6.cloned.1.call-done = f32[64,64,3,3]{1,0,3,2:T(8,128)} async-done(((f32[64,64,3,3]{1,0,3,2:T(8,128)}), f32[64,64,3,3]{1,0,3,2:T(8,128)}) %all-reduce.6.cloned.1.call-update) | async-done | bytes 147472 | tf_op jit(solution)/shard_map/psum | solution.py:155
  296.0 1.7 copy.226
  298.9 1.4 copy.228
  300.3 1.4 copy.229
  301.7 1.4 copy.230
  303.0 1.4 copy.231
  (243 shorter events, 43.5 us)
Async XLA Ops:
  7.2 5.0 %copy-start.2 = (bf16[64,73,2,16]{1,3,2,0:T(8,128)(2,1)S(1)}, bf16[64,73,2,16]{1,3,2,0:T(8,128)(2,1)}, u32[]{:S(2)}) copy-start(bf16[64,73,2,16]{1,3,2,0:T(8,128)(2,1)} %param.11) | copy-start | bytes 897028
  7.2 5.0 %copy-start.13 = (bf16[64,64,3,3]{1,0,3,2:T(8,128)(2,1)S(1)}, bf16[64,64,3,3]{1,0,3,2:T(8,128)(2,1)}, u32[]{:S(2)}) copy-start(bf16[64,64,3,3]{1,0,3,2:T(8,128)(2,1)} %param.14) | copy-start | bytes 221188
  8.4 4.1 %collective-permute-start = (bf16[64,73,1,16]{1,0,3,2:T(8,128)(2,1)S(1)}, bf16[64,73,1,16]{1,0,3,2:T(8,128)(2,1)S(1)}, u32[]{:S(2)}, u32[]{:S(2)}) collective-permute-start(bf16[64,73,1,16]{1,0,3,2:T(8,128)(2,1)S(1)} %copy.172), channel_id=1, source_target_pairs={{0,1},{1,2},{2,3},{4,5},{5,6},{6,7},{8,9},{9,10},{10,11},{12,13},{... | collective-permute-start | bytes 448520 | tf_op jit(solution)/shard_map/ppermute | solution.py:16
  10.9 5.5 %collective-permute-start.1 = (bf16[64,73,1,16]{1,0,3,2:T(8,128)(2,1)S(1)}, bf16[64,73,1,16]{1,0,3,2:T(8,128)(2,1)S(1)}, u32[]{:S(2)}, u32[]{:S(2)}) collective-permute-start(bf16[64,73,1,16]{1,0,3,2:T(8,128)(2,1)S(1)} %copy.173), channel_id=1, source_target_pairs={{1,0},{2,1},{3,2},{5,4},{6,5},{7,6},{9,8},{10,9},{11,10},{13,12},{... | collective-permute-start | bytes 448520 | tf_op jit(solution)/shard_map/ppermute | solution.py:18
  19.1 5.9 %copy-start.18 = (bf16[64,292,2,4]{1,3,2,0:T(4,128)(2,1)S(1)}, bf16[64,292,2,4]{1,3,2,0:T(4,128)(2,1)}, u32[]{:S(2)}) copy-start(bf16[64,292,2,4]{1,3,2,0:T(4,128)(2,1)} %param.12) | copy-start | bytes 897028
  20.0 18.2 %copy-start.12 = (bf16[64,64]{1,0:T(8,128)(2,1)S(1)}, bf16[64,64]{1,0:T(8,128)(2,1)}, u32[]{:S(2)}) copy-start(bf16[64,64]{1,0:T(8,128)(2,1)} %param.19) | copy-start | bytes 24580
  20.0 18.2 %copy-start.15 = (bf16[64,64]{1,0:T(8,128)(2,1)S(1)}, bf16[64,64]{1,0:T(8,128)(2,1)}, u32[]{:S(2)}) copy-start(bf16[64,64]{1,0:T(8,128)(2,1)} %param.18) | copy-start | bytes 24580
  20.0 18.2 %copy-start.34 = (f32[64]{0:T(128)S(1)}, f32[64]{0:T(128)}, u32[]{:S(2)}) copy-start(f32[64]{0:T(128)} %param.15) | copy-start | bytes 772
  20.0 17.4 %all-to-all-start = ((bf16[64,73,2,4,4]{1,0,4,2,3:T(8,128)(2,1)}), bf16[64,73,2,4,4]{1,0,4,2,3:T(8,128)(2,1)S(1)}, u32[]{:S(2)}, u32[]{:S(2)}) async-start(bf16[64,73,2,4,4]{1,0,4,2,3:T(8,128)(2,1)} %copy.93), calls=%async_computation | async-start | bytes 1048576 | tf_op jit(solution)/shard_map/all_to_all | solution.py:131
  46.0 9.2 %copy-start.42 = (f32[4,292]{1,0:T(4,128)}, f32[4,292]{1,0:T(4,128)S(1)}, u32[]{:S(2)}) copy-start(f32[4,292]{1,0:T(4,128)S(1)} %get-tuple-element.289) | copy-start | bytes 14020 | tf_op jit(solution)/shard_map/while
  57.4 5.1 %copy-start.5 = (bf16[4,292,64]{1,2,0:T(8,128)(2,1)S(1)}, bf16[4,292,64]{1,2,0:T(8,128)(2,1)}, u32[]{:S(2)}) copy-start(bf16[4,292,64]{1,2,0:T(8,128)(2,1)} %copy-done.4) | copy-start | bytes 448516 | tf_op jit(solution)/shard_map/while
  57.4 5.1 %copy-start.43 = (f32[4,292]{1,0:T(4,128)S(1)}, f32[4,292]{1,0:T(4,128)}, u32[]{:S(2)}) copy-start(f32[4,292]{1,0:T(4,128)} %copy-done.42) | copy-start | bytes 14020 | tf_op jit(solution)/shard_map/while
  59.5 4.9 %copy-start.20 = (bf16[2,4,292,64]{2,3,1,0:T(8,128)(2,1)}, bf16[2,4,292,64]{2,3,1,0:T(8,128)(2,1)S(1)}, u32[]{:S(2)}) copy-start(bf16[2,4,292,64]{2,3,1,0:T(8,128)(2,1)S(1)} %fusion.295) | copy-start | bytes 897028 | tf_op jit(solution)/shard_map/while
  59.6 4.8 %copy-start.38 = (f32[2,64]{1,0:T(2,128)}, f32[2,64]{1,0:T(2,128)S(1)}, u32[]{:S(2)}) copy-start(f32[2,64]{1,0:T(2,128)S(1)} %dynamic_update_slice.43) | copy-start | bytes 1540 | tf_op jit(solution)/shard_map/while
  66.7 4.5 %copy-start.36 = (s32[292]{0:T(512)S(1)}, s32[292]{0:T(512)}, u32[]{:S(2)}) copy-start(s32[292]{0:T(512)} %get-tuple-element.341) | copy-start | bytes 3508 | tf_op jit(solution)/shard_map/while
  66.7 4.5 %copy-start.17 = (bf16[64,64]{1,0:T(8,128)(2,1)S(1)}, bf16[64,64]{1,0:T(8,128)(2,1)}, u32[]{:S(2)}) copy-start(bf16[64,64]{1,0:T(8,128)(2,1)} %get-tuple-element.343) | copy-start | bytes 24580 | tf_op jit(solution)/shard_map/while
  74.3 9.2 %copy-start.42 = (f32[4,292]{1,0:T(4,128)}, f32[4,292]{1,0:T(4,128)S(1)}, u32[]{:S(2)}) copy-start(f32[4,292]{1,0:T(4,128)S(1)} %get-tuple-element.289) | copy-start | bytes 14020 | tf_op jit(solution)/shard_map/while
  85.7 5.1 %copy-start.5 = (bf16[4,292,64]{1,2,0:T(8,128)(2,1)S(1)}, bf16[4,292,64]{1,2,0:T(8,128)(2,1)}, u32[]{:S(2)}) copy-start(bf16[4,292,64]{1,2,0:T(8,128)(2,1)} %copy-done.4) | copy-start | bytes 448516 | tf_op jit(solution)/shard_map/while
  85.7 5.1 %copy-start.43 = (f32[4,292]{1,0:T(4,128)S(1)}, f32[4,292]{1,0:T(4,128)}, u32[]{:S(2)}) copy-start(f32[4,292]{1,0:T(4,128)} %copy-done.42) | copy-start | bytes 14020 | tf_op jit(solution)/shard_map/while
  87.8 4.9 %copy-start.20 = (bf16[2,4,292,64]{2,3,1,0:T(8,128)(2,1)}, bf16[2,4,292,64]{2,3,1,0:T(8,128)(2,1)S(1)}, u32[]{:S(2)}) copy-start(bf16[2,4,292,64]{2,3,1,0:T(8,128)(2,1)S(1)} %fusion.295) | copy-start | bytes 897028 | tf_op jit(solution)/shard_map/while
  87.9 4.8 %copy-start.38 = (f32[2,64]{1,0:T(2,128)}, f32[2,64]{1,0:T(2,128)S(1)}, u32[]{:S(2)}) copy-start(f32[2,64]{1,0:T(2,128)S(1)} %dynamic_update_slice.43) | copy-start | bytes 1540 | tf_op jit(solution)/shard_map/while
  94.8 8.2 %copy-start.27 = (f32[2,64,64]{2,1,0:T(8,128)S(1)}, f32[2,64,64]{2,1,0:T(8,128)}, u32[]{:S(2)}) copy-start(f32[2,64,64]{2,1,0:T(8,128)} %get-tuple-element.410) | copy-start | bytes 98308
  94.8 8.8 %copy-start.30 = (f32[2,64,64]{2,1,0:T(8,128)S(1)}, f32[2,64,64]{2,1,0:T(8,128)}, u32[]{:S(2)}) copy-start(f32[2,64,64]{2,1,0:T(8,128)} %get-tuple-element.411) | copy-start | bytes 98308
  94.8 9.4 %copy-start.33 = (f32[2,64,64]{2,1,0:T(8,128)S(1)}, f32[2,64,64]{2,1,0:T(8,128)}, u32[]{:S(2)}) copy-start(f32[2,64,64]{2,1,0:T(8,128)} %get-tuple-element.412) | copy-start | bytes 98308
  94.8 10.1 %copy-start.24 = (f32[2,64,64]{2,1,0:T(8,128)S(1)}, f32[2,64,64]{2,1,0:T(8,128)}, u32[]{:S(2)}) copy-start(f32[2,64,64]{2,1,0:T(8,128)} %get-tuple-element.413) | copy-start | bytes 98308
  94.8 10.7 %copy-start.39 = (f32[2,64]{1,0:T(2,128)S(1)}, f32[2,64]{1,0:T(2,128)}, u32[]{:S(2)}) copy-start(f32[2,64]{1,0:T(2,128)} %get-tuple-element.409) | copy-start | bytes 1540
  97.8 14.7 %all-to-all-start.1 = ((bf16[4,2,18688]{2,1,0:T(2,128)(2,1)}), bf16[4,2,18688]{2,1,0:T(2,128)(2,1)S(1)}, u32[]{:S(2)}, u32[]{:S(2)}) async-start(bf16[4,2,18688]{2,1,0:T(2,128)(2,1)} %reshape.106), calls=%async_computation.1 | async-start | bytes 598016 | tf_op jit(solution)/shard_map/all_to_all | solution.py:142
  103.0 96.1 %all-reduce.8.cloned.1.call-start = ((), (), s32[]{:S(2)}) async-start(), calls=%async_computation.3 | async-start | bytes 263168 | tf_op jit(solution)/shard_map/psum | solution.py:155
  106.0 190.0 %all-reduce.6.cloned.1.call-start = ((), (), s32[]{:S(2)}) async-start(), calls=%async_computation.2 | async-start | bytes 589824 | tf_op jit(solution)/shard_map/psum | solution.py:155
  117.4 5.3 %copy-start.21 = (f32[64,64,9]{1,0,2:T(8,128)}, f32[64,64,9]{1,0,2:T(8,128)S(1)}, u32[]{:S(2)}) copy-start(f32[64,64,9]{1,0,2:T(8,128)S(1)} %fusion.104) | copy-start | bytes 442372
  117.4 5.6 %collective-permute-start.3 = (bf16[64,73,1,16]{1,0,3,2:T(8,128)(2,1)S(1)}, bf16[64,73,1,16]{1,0,3,2:T(8,128)(2,1)S(1)}, u32[]{:S(2)}, u32[]{:S(2)}) collective-permute-start(bf16[64,73,1,16]{1,0,3,2:T(8,128)(2,1)S(1)} %get-tuple-element.173), channel_id=1, source_target_pairs={{1,0},{2,1},{3,2},{5,4},{6,5},{7,6},{9,8},{10,9},{11,10},{13,12},{... | collective-permute-start | bytes 448520 | tf_op jit(solution)/shard_map/ppermute | solution.py:18
  118.7 5.1 %collective-permute-start.2 = (bf16[64,73,1,16]{1,0,3,2:T(8,128)(2,1)S(1)}, bf16[64,73,1,16]{1,0,3,2:T(8,128)(2,1)S(1)}, u32[]{:S(2)}, u32[]{:S(2)}) collective-permute-start(bf16[64,73,1,16]{1,0,3,2:T(8,128)(2,1)S(1)} %get-tuple-element.172), channel_id=1, source_target_pairs={{0,1},{1,2},{2,3},{4,5},{5,6},{6,7},{8,9},{9,10},{10,11},{12,13},{... | collective-permute-start | bytes 448520 | tf_op jit(solution)/shard_map/ppermute | solution.py:16
  (47 other events, 123.4 us)
Sparse Core Ops, SparseCore 0:
  108.4 90.5 all-reduce.7
  203.0 93.0 all-reduce.5
where the time goes:
time: 313 us; the launch traced here: 311 us
  waiting for transfers between devices  191 us (61%)
  matrix products  58.5 us (19%)
  local copies, waits for them, and re-layouts  22.2 us (7%)
  starting transfers between devices  19.4 us (6%)
  between operations  14.6 us (5%)
  other arithmetic  5.07 us (2%)
    psum x2, waiting for transfers between devices, body(): lax.psum((g_conv, g_gain, g_query, g_key, g_value, g_out), ('view', 'row'))  168 us
    dot_general x59, matrix products, product(): return jnp.einsum(form, left, right, preferred_element_type=jnp.float32)  52.2 us
    unnamed x48, local copies, waits for them, and re-layouts  12.6 us
    all_to_all x1, waiting for transfers between devices, body(): lax.all_to_all(spatial.reshape(channels, view_dev, row_dev, blocks, bread...  12.3 us
    ppermute x2, starting transfers between devices, with_halo(): lax.ppermute(tail, axis, [(i, (i + 1) % count) for i in range(ends)])  6.37 us
  transfers between devices with their start and end apart: 8, of which 6 were waited for; matrix products, arithmetic and copies ran while one was open for 4% of the time, Pallas kernels for 0%

commit v1 on v0

--- a/solution.py
+++ b/solution.py
@@ -3,6 +3,22 @@
 import jax.numpy as jnp
 from jax import lax
 from jax.sharding import PartitionSpec as P
+
+
+def swapped_with_each(shard, axis, split, join):
+    ways, here = (lax.axis_size(axis), lax.axis_index(axis))
+    width = shard.shape[split] // ways
+    shape = list(shard.shape)
+    shape[split] = width
+    height = shape[join]
+    shape[join] = height * ways
+    full = jnp.zeros(shape, shard.dtype)
+    for mask in range(ways):
+        part = lax.dynamic_slice_in_dim(shard, (here ^ mask) * width, width, axis=split)
+        if mask:
+            part = lax.ppermute(part, axis, [(d, d ^ mask) for d in range(ways)])
+        full = lax.dynamic_update_slice_in_dim(full, part, (here ^ mask) * height, axis=join)
+    return full
 
 
 def with_halo(cells, sides, width):
@@ -128,12 +144,8 @@
     padded = with_halo(inputs, (("row", 2),), 1)
     padded = jnp.pad(padded, ((0, 0), (0, 0), (0, 0), (1, 1)))
     spatial = (inputs.astype(jnp.float32) + convolve(padded, w_conv)).astype(jnp.bfloat16)
-    moved = lax.all_to_all(
-        spatial.reshape(channels, view_dev, row_dev, blocks, breadth),
-        "view",
-        split_axis=3,
-        concat_axis=1,
-        tiled=True,
+    moved = swapped_with_each(
+        spatial.reshape(channels, view_dev, row_dev, blocks, breadth), "view", 3, 1
     )
     moved = moved.reshape(channels, all_views, row_dev, breadth)
     output, d_spatial, grads = angular_rows(

time: 313 us -> 301 us (0.962)
  waiting for transfers between devices: 191 us -> 182 us
  matrix products: 58.5 us -> 52.7 us
  local copies, waits for them, and re-layouts: 22.2 us -> 25.7 us
    all_to_all x1 -> x0, waiting for transfers between devices: 12.3 us -> none  [body(): lax.all_to_all(spatial.reshape(channels, view_dev, row_dev, blocks, bread...]
    dynamic_update_slice x0 -> x4, local copies, waits for them, and re-layouts: none -> 6.17 us  [swapped_with_each(): lax.dynamic_update_slice_in_dim(full, part, (here ^ mask) * height, axis=...]
    dot_general x59, matrix products: 52.2 us -> 46.5 us  [product(): return jnp.einsum(form, left, right, preferred_element_type=jnp.float32)]
    all_to_all x1 -> x0, starting transfers between devices: 5 us -> none  [body(): lax.all_to_all(spatial.reshape(channels, view_dev, row_dev, blocks, bread...]
    ppermute x0 -> x3, starting transfers between devices: none -> 4.45 us  [swapped_with_each(): part = lax.ppermute(part, axis, [(d, d ^ mask) for d in range(ways)])]
    ppermute x0 -> x3, waiting for transfers between devices: none -> 3.51 us  [swapped_with_each(): part = lax.ppermute(part, axis, [(d, d ^ mask) for d in range(ways)])]
    unnamed x48 -> x51, local copies, waits for them, and re-layouts: 12.6 us -> 12.6 us
  transfers between devices with their start and end apart: 8 -> 10, of which waited for: 6 -> 7; matrix products, arithmetic and copies ran while one was open for 4% -> 6% of each run, Pallas kernels for 0% -> 0%
where the time goes in v1:
time: 301 us; the launch traced here: 300 us
  waiting for transfers between devices  182 us (60%)
  matrix products  52.7 us (18%)
  local copies, waits for them, and re-layouts  25.7 us (9%)
  starting transfers between devices  19.9 us (7%)
  between operations  14.7 us (5%)
  other arithmetic  4.59 us (2%)
    psum x2, waiting for transfers between devices, body(): lax.psum((g_conv, g_gain, g_query, g_key, g_value, g_out), ('view', 'row'))  169 us
    dot_general x59, matrix products, product(): return jnp.einsum(form, left, right, preferred_element_type=jnp.float32)  46.5 us
    unnamed x51, local copies, waits for them, and re-layouts  12.6 us
    ppermute x2, starting transfers between devices, with_halo(): lax.ppermute(tail, axis, [(i, (i + 1) % count) for i in range(ends)])  6.8 us
    sub x2, matrix products, angular(): expo = jnp.exp(scores - highest)  6.21 us
    dynamic_update_slice x4, local copies, waits for them, and re-layouts, swapped_with_each(): lax.dynamic_update_slice_in_dim(full, part, (here ^ mask) * height, axis=...  6.17 us
  transfers between devices with their start and end apart: 10, of which 7 were waited for; matrix products, arithmetic and copies ran while one was open for 6% of the time, Pallas kernels for 0%

profile of v1, /device:TPU:0, one launch (start us, length us, event | category | flops | bytes accessed | tf_op | source)
XLA Modules:
  0.0 299.8 jit_solution(4222755778860136603)
XLA Ops:
  8.4 2.4 collective-permute-start
  13.2 3.2 %collective-permute-done.1 = bf16[64,73,1,16]{1,0,3,2:T(8,128)(2,1)S(1)} collective-permute-done((bf16[64,73,1,16]{1,0,3,2:T(8,128)(2,1)S(1)}, bf16[64,73,1,16]{1,0,3,2:T(8,128)(2,1)S(1)}, u32[]{:S(2)}, u32[]{:S(2)}) %collective-permute-start.1) | collective-permute-done | bytes 149536 | tf_op jit(solution)/shard_map/ppermute | solution.py:34
  19.2 1.6 collective-permute-start.2
  20.9 2.6 collective-permute-start.3
  24.6 1.8 dynamic_update_slice.41
  26.4 1.8 collective-permute-done.3
  28.2 1.8 dynamic_update_slice.42
  30.1 1.7 collective-permute-done.4
  31.7 1.8 dynamic_update_slice.43
  33.6 48.1 %while.22 = (s32[]{:T(128)}, bf16[2,4,292,64]{2,1,0,3:T(4,128)(2,1)}, bf16[2,4,292,64]{2,3,1,0:T(8,128)(2,1)}, f32[2,64]{1,0:T(2,128)S(1)}, f32[2,64,64]{2,1,0:T...) while((s32[]{:T(128)}, ...), condition=%wide.region_9.10_spmd, body=%wide.region_0.9_spmd.sunk | while | flops 399432576 | bytes 35000580 | solution.py:134
  35.2 1.5 fusion.290
  37.7 3.1 %fusion.288 = (f32[4,292]{1,0:T(4,128)S(1)}, f32[4,292,292]{1,2,0:T(8,128)}) fusion(pred[292]{0:T(512)(128)(4,1)S(1)} %broadcast_compare_fusion.2, bf16[4,292,64]{1,2,0:T(8,128)(2,1)} %convolution_convert_fusion.12, bf16[64,64]{1,0:T(8,128)(2,1)S(1)} %get-tuple-element.339, f32[64]{0:T(128)S(1)} %get-tuple-element.338, ...), kind=kOutput, calls=%fused_computation.197.clone.1 | convolution fusion | flops 55036452 | bytes 1744708 | tf_op jit(solution)/shard_map/while/body/eval_jaxpr/sub | solution.py:95
  40.8 3.5 %fusion.293 = bf16[4,292,64]{1,2,0:T(8,128)(2,1)} fusion(f32[4,292,292]{1,2,0:T(8,128)S(1)} %fusion.290, f32[4,292,292]{1,2,0:T(8,128)} %get-tuple-element.284, f32[4,292]{1,0:T(4,128)S(1)} %get-tuple-element.285, bf16[64,64]{1,0:T(8,128)(2,1)S(1)} %get-tuple-element.339, f32[64]{0:T(128)S(1)} %get-tuple-element.338, ...), kind=kOutput, calls=%fused_computation.14.clone.1 | convolution fusion | flops 56135540 | bytes 7662592 | tf_op jit(solution)/shard_map/while/body/eval_jaxpr/pvu,pvd->pud/dot_general | solution.py:42
  44.3 3.5 %fusion.291 = bf16[4,292,64]{1,2,0:T(8,128)(2,1)} fusion(bf16[4,292,64]{1,2,0:T(8,128)(2,1)} %convolution_convert_fusion.12, f32[4,292,292]{1,2,0:T(8,128)S(1)} %fusion.290, f32[4,292,292]{1,2,0:T(8,128)} %get-tuple-element.284, f32[4,292]{1,0:T(4,128)S(1)} %get-tuple-element.285), kind=kOutput, calls=%fused_computation.13.clone.1 | convolution fusion | flops 46118772 | bytes 3032128 | tf_op jit(solution)/shard_map/while/body/eval_jaxpr/pvu,pud->pvd/dot_general | solution.py:42
  50.0 2.0 convolution_convert_fusion.15
  54.4 1.9 convolution_convert_fusion.13
  59.3 1.5 fusion.290
  61.7 3.1 %fusion.288 = (f32[4,292]{1,0:T(4,128)S(1)}, f32[4,292,292]{1,2,0:T(8,128)}) fusion(pred[292]{0:T(512)(128)(4,1)S(1)} %broadcast_compare_fusion.2, bf16[4,292,64]{1,2,0:T(8,128)(2,1)} %convolution_convert_fusion.12, bf16[64,64]{1,0:T(8,128)(2,1)S(1)} %get-tuple-element.339, f32[64]{0:T(128)S(1)} %get-tuple-element.338, ...), kind=kOutput, calls=%fused_computation.197.clone.1 | convolution fusion | flops 55036452 | bytes 1744708 | tf_op jit(solution)/shard_map/while/body/eval_jaxpr/sub | solution.py:95
  64.8 3.5 %fusion.293 = bf16[4,292,64]{1,2,0:T(8,128)(2,1)} fusion(f32[4,292,292]{1,2,0:T(8,128)S(1)} %fusion.290, f32[4,292,292]{1,2,0:T(8,128)} %get-tuple-element.284, f32[4,292]{1,0:T(4,128)S(1)} %get-tuple-element.285, bf16[64,64]{1,0:T(8,128)(2,1)S(1)} %get-tuple-element.339, f32[64]{0:T(128)S(1)} %get-tuple-element.338, ...), kind=kOutput, calls=%fused_computation.14.clone.1 | convolution fusion | flops 56135540 | bytes 7662592 | tf_op jit(solution)/shard_map/while/body/eval_jaxpr/pvu,pvd->pud/dot_general | solution.py:42
  68.3 3.5 %fusion.291 = bf16[4,292,64]{1,2,0:T(8,128)(2,1)} fusion(bf16[4,292,64]{1,2,0:T(8,128)(2,1)} %convolution_convert_fusion.12, f32[4,292,292]{1,2,0:T(8,128)S(1)} %fusion.290, f32[4,292,292]{1,2,0:T(8,128)} %get-tuple-element.284, f32[4,292]{1,0:T(4,128)S(1)} %get-tuple-element.285), kind=kOutput, calls=%fused_computation.13.clone.1 | convolution fusion | flops 46118772 | bytes 3032128 | tf_op jit(solution)/shard_map/while/body/eval_jaxpr/pvu,pud->pvd/dot_general | solution.py:42
  74.1 2.0 convolution_convert_fusion.15
  78.5 1.9 convolution_convert_fusion.13
  81.7 1.6 copy.69
  84.6 6.0 %all-to-all-start = ((bf16[4,2,18688]{2,1,0:T(2,128)(2,1)}), bf16[4,2,18688]{2,1,0:T(2,128)(2,1)S(1)}, u32[]{:S(2)}, u32[]{:S(2)}) async-start(bf16[4,2,18688]{2,1,0:T(2,128)(2,1)} %reshape.125), calls=%async_computation | async-start | bytes 598016 | tf_op jit(solution)/shard_map/all_to_all | solution.py:154
  91.8 1.5 reduce_sum.111
  94.5 5.4 %all-to-all-done = bf16[4,2,18688]{2,1,0:T(2,128)(2,1)S(1)} async-done(((bf16[4,2,18688]{2,1,0:T(2,128)(2,1)}), bf16[4,2,18688]{2,1,0:T(2,128)(2,1)S(1)}, u32[]{:S(2)}, u32[]{:S(2)}) %all-to-all-start) | async-done | bytes 299040 | tf_op jit(solution)/shard_map/all_to_all | solution.py:154
  106.1 4.4 %collective-permute-start.5 = (bf16[64,73,1,16]{1,0,3,2:T(8,128)(2,1)S(1)}, bf16[64,73,1,16]{1,0,3,2:T(8,128)(2,1)S(1)}, u32[]{:S(2)}, u32[]{:S(2)}) collective-permute-start(bf16[64,73,1,16]{1,0,3,2:T(8,128)(2,1)S(1)} %get-tuple-element.164), channel_id=1, source_target_pairs={{0,1},{1,2},{2,3},{4,5},{5,6},{6,7},{8,9},{9,10},{10,11},{12,13},{... | collective-permute-start | bytes 448520 | tf_op jit(solution)/shard_map/ppermute | solution.py:32
  115.3 72.4 %all-reduce.8.cloned.1.call-done = (f32[64]{0:T(128)}, f32[64,64]{1,0:T(8,128)}, f32[64,64]{1,0:T(8,128)}, f32[64,64]{1,0:T(8,128)}, f32[64,64]{1,0:T(8,128)}) async-done(((f32[64]{0:T(128)}, f32[64,64]{1,0:T(8,128)}, f32[64,64]{1,0:T(8,128)}, f32[64,64]{1,0:T(8,128)}, f32[64,64]{1,0:T(8,128)}), (f32[64]{0:T(128)}, f32[64,64]{1,0:T(8,128)}, f32[64,64]{1,0:T(8,128)}, f32[64,64]{1,0:T(8,128)}, ...) | async-done | bytes 65808 | tf_op jit(solution)/shard_map/psum | solution.py:167
  187.6 97.0 %all-reduce.6.cloned.1.call-done = f32[64,64,3,3]{1,0,3,2:T(8,128)} async-done(((f32[64,64,3,3]{1,0,3,2:T(8,128)}), f32[64,64,3,3]{1,0,3,2:T(8,128)}) %all-reduce.6.cloned.1.call-update) | async-done | bytes 147472 | tf_op jit(solution)/shard_map/psum | solution.py:167
  284.6 1.7 copy.205
  287.4 1.4 copy.207
  288.8 1.4 copy.208
  (208 shorter events, 42.3 us)
Async XLA Ops:
  7.2 5.1 %copy-start.2 = (bf16[64,73,2,16]{1,3,2,0:T(8,128)(2,1)S(1)}, bf16[64,73,2,16]{1,3,2,0:T(8,128)(2,1)}, u32[]{:S(2)}) copy-start(bf16[64,73,2,16]{1,3,2,0:T(8,128)(2,1)} %param.11) | copy-start | bytes 897028
  7.2 5.1 %copy-start.13 = (bf16[64,64,3,3]{1,0,3,2:T(8,128)(2,1)S(1)}, bf16[64,64,3,3]{1,0,3,2:T(8,128)(2,1)}, u32[]{:S(2)}) copy-start(bf16[64,64,3,3]{1,0,3,2:T(8,128)(2,1)} %param.14) | copy-start | bytes 221188
  8.4 4.2 %collective-permute-start = (bf16[64,73,1,16]{1,0,3,2:T(8,128)(2,1)S(1)}, bf16[64,73,1,16]{1,0,3,2:T(8,128)(2,1)S(1)}, u32[]{:S(2)}, u32[]{:S(2)}) collective-permute-start(bf16[64,73,1,16]{1,0,3,2:T(8,128)(2,1)S(1)} %copy.147), channel_id=1, source_target_pairs={{0,1},{1,2},{2,3},{4,5},{5,6},{6,7},{8,9},{9,10},{10,11},{12,13},{... | collective-permute-start | bytes 448520 | tf_op jit(solution)/shard_map/ppermute | solution.py:32
  10.9 5.5 %collective-permute-start.1 = (bf16[64,73,1,16]{1,0,3,2:T(8,128)(2,1)S(1)}, bf16[64,73,1,16]{1,0,3,2:T(8,128)(2,1)S(1)}, u32[]{:S(2)}, u32[]{:S(2)}) collective-permute-start(bf16[64,73,1,16]{1,0,3,2:T(8,128)(2,1)S(1)} %copy.148), channel_id=1, source_target_pairs={{1,0},{2,1},{3,2},{5,4},{6,5},{7,6},{9,8},{10,9},{11,10},{13,12},{... | collective-permute-start | bytes 448520 | tf_op jit(solution)/shard_map/ppermute | solution.py:34
  13.2 4.2 %copy-start.10 = (bf16[64,73,3,16]{1,0,3,2:T(8,128)(2,1)}, bf16[64,73,3,16]{1,0,3,2:T(8,128)(2,1)S(1)}, u32[]{:S(2)}) copy-start(bf16[64,73,3,16]{1,0,3,2:T(8,128)(2,1)S(1)} %get-tuple-element.170) | copy-start | bytes 1345540
  18.6 5.1 %copy-start.17 = (bf16[64,292,2,4]{1,3,2,0:T(4,128)(2,1)S(1)}, bf16[64,292,2,4]{1,3,2,0:T(4,128)(2,1)}, u32[]{:S(2)}) copy-start(bf16[64,292,2,4]{1,3,2,0:T(4,128)(2,1)} %param.12) | copy-start | bytes 897028
  19.1 14.4 %copy-start.12 = (bf16[64,64]{1,0:T(8,128)(2,1)S(1)}, bf16[64,64]{1,0:T(8,128)(2,1)}, u32[]{:S(2)}) copy-start(bf16[64,64]{1,0:T(8,128)(2,1)} %param.19) | copy-start | bytes 24580
  19.1 14.4 %copy-start.14 = (bf16[64,64]{1,0:T(8,128)(2,1)S(1)}, bf16[64,64]{1,0:T(8,128)(2,1)}, u32[]{:S(2)}) copy-start(bf16[64,64]{1,0:T(8,128)(2,1)} %param.17) | copy-start | bytes 24580
  19.1 14.4 %copy-start.15 = (bf16[64,64]{1,0:T(8,128)(2,1)S(1)}, bf16[64,64]{1,0:T(8,128)(2,1)}, u32[]{:S(2)}) copy-start(bf16[64,64]{1,0:T(8,128)(2,1)} %param.18) | copy-start | bytes 24580
  19.1 14.4 %copy-start.16 = (bf16[64,64]{1,0:T(8,128)(2,1)S(1)}, bf16[64,64]{1,0:T(8,128)(2,1)}, u32[]{:S(2)}) copy-start(bf16[64,64]{1,0:T(8,128)(2,1)} %param.16) | copy-start | bytes 24580
  19.2 14.4 %copy-start.30 = (f32[64]{0:T(128)S(1)}, f32[64]{0:T(128)}, u32[]{:S(2)}) copy-start(f32[64]{0:T(128)} %param.15) | copy-start | bytes 772
  19.2 14.4 %copy-start.31 = (s32[292]{0:T(512)S(1)}, s32[292]{0:T(512)}, u32[]{:S(2)}) copy-start(s32[292]{0:T(512)} %param.13) | copy-start | bytes 3508
  19.2 5.3 %collective-permute-start.2 = (bf16[64,73,2,1,4]{1,0,4,2,3:T(8,128)(2,1)S(1)}, bf16[64,73,2,1,4]{1,0,4,2,3:T(8,128)(2,1)S(1)}, u32[]{:S(2)}, u32[]{:S(2)}) collective-permute-start(bf16[64,73,2,1,4]{1,0,4,2,3:T(8,128)(2,1)S(1)} %get-tuple-element.168), channel_id=1, source_target_pairs={{0,4},{4,0},{8,12},{12,8},{1,5},{5,1},{9,13},{13,9},{2,6},{6,2},{1... | collective-permute-start | bytes 224264 | tf_op jit(solution)/shard_map/ppermute | solution.py:19
  20.9 7.4 %collective-permute-start.3 = (bf16[64,73,2,1,4]{1,0,4,2,3:T(8,128)(2,1)S(1)}, bf16[64,73,2,1,4]{1,0,4,2,3:T(8,128)(2,1)S(1)}, u32[]{:S(2)}, u32[]{:S(2)}) collective-permute-start(bf16[64,73,2,1,4]{1,0,4,2,3:T(8,128)(2,1)S(1)} %get-tuple-element.167), channel_id=1, source_target_pairs={{0,8},{4,12},{8,0},{12,4},{1,9},{5,13},{9,1},{13,5},{2,10},{6,14},... | collective-permute-start | bytes 224264 | tf_op jit(solution)/shard_map/ppermute | solution.py:19
  23.5 8.3 %collective-permute-start.4 = (bf16[64,73,2,1,4]{1,0,4,2,3:T(8,128)(2,1)S(1)}, bf16[64,73,2,1,4]{1,0,4,2,3:T(8,128)(2,1)S(1)}, u32[]{:S(2)}, u32[]{:S(2)}) collective-permute-start(bf16[64,73,2,1,4]{1,0,4,2,3:T(8,128)(2,1)S(1)} %get-tuple-element.166), channel_id=1, source_target_pairs={{0,12},{4,8},{8,4},{12,0},{1,13},{5,9},{9,5},{13,1},{2,14},{6,10},... | collective-permute-start | bytes 224264 | tf_op jit(solution)/shard_map/ppermute | solution.py:19
  52.7 4.3 %copy-start.19 = (bf16[2,4,292,64]{2,3,1,0:T(8,128)(2,1)}, bf16[2,4,292,64]{2,3,1,0:T(8,128)(2,1)S(1)}, u32[]{:S(2)}) copy-start(bf16[2,4,292,64]{2,3,1,0:T(8,128)(2,1)S(1)} %fusion.295) | copy-start | bytes 897028 | tf_op jit(solution)/shard_map/while
  53.3 3.1 %copy-start.28 = (f32[2,64,64]{2,1,0:T(8,128)}, f32[2,64,64]{2,1,0:T(8,128)S(1)}, u32[]{:S(2)}) copy-start(f32[2,64,64]{2,1,0:T(8,128)S(1)} %fusion.297) | copy-start | bytes 98308 | tf_op jit(solution)/shard_map/while
  53.5 2.8 copy-start.25
  74.1 2.5 copy-start.1
  74.1 2.5 copy-start.18
  76.8 4.3 %copy-start.19 = (bf16[2,4,292,64]{2,3,1,0:T(8,128)(2,1)}, bf16[2,4,292,64]{2,3,1,0:T(8,128)(2,1)S(1)}, u32[]{:S(2)}) copy-start(bf16[2,4,292,64]{2,3,1,0:T(8,128)(2,1)S(1)} %fusion.295) | copy-start | bytes 897028 | tf_op jit(solution)/shard_map/while
  77.3 3.1 %copy-start.28 = (f32[2,64,64]{2,1,0:T(8,128)}, f32[2,64,64]{2,1,0:T(8,128)S(1)}, u32[]{:S(2)}) copy-start(f32[2,64,64]{2,1,0:T(8,128)S(1)} %fusion.297) | copy-start | bytes 98308 | tf_op jit(solution)/shard_map/while
  77.6 2.8 copy-start.25
  81.7 8.9 %copy-start.26 = (f32[2,64,64]{2,1,0:T(8,128)S(1)}, f32[2,64,64]{2,1,0:T(8,128)}, u32[]{:S(2)}) copy-start(f32[2,64,64]{2,1,0:T(8,128)} %get-tuple-element.99) | copy-start | bytes 98308
  81.7 9.5 %copy-start.29 = (f32[2,64,64]{2,1,0:T(8,128)S(1)}, f32[2,64,64]{2,1,0:T(8,128)}, u32[]{:S(2)}) copy-start(f32[2,64,64]{2,1,0:T(8,128)} %get-tuple-element.100) | copy-start | bytes 98308
  81.7 11.6 %copy-start.23 = (f32[2,64,64]{2,1,0:T(8,128)S(1)}, f32[2,64,64]{2,1,0:T(8,128)}, u32[]{:S(2)}) copy-start(f32[2,64,64]{2,1,0:T(8,128)} %get-tuple-element.102) | copy-start | bytes 98308
  84.6 15.3 %all-to-all-start = ((bf16[4,2,18688]{2,1,0:T(2,128)(2,1)}), bf16[4,2,18688]{2,1,0:T(2,128)(2,1)S(1)}, u32[]{:S(2)}, u32[]{:S(2)}) async-start(bf16[4,2,18688]{2,1,0:T(2,128)(2,1)} %reshape.125), calls=%async_computation | async-start | bytes 598016 | tf_op jit(solution)/shard_map/all_to_all | solution.py:154
  90.6 97.0 %all-reduce.8.cloned.1.call-start = ((), (), s32[]{:S(2)}) async-start(), calls=%async_computation.2 | async-start | bytes 263168 | tf_op jit(solution)/shard_map/psum | solution.py:167
  94.5 190.1 %all-reduce.6.cloned.1.call-start = ((), (), s32[]{:S(2)}) async-start(), calls=%async_computation.1 | async-start | bytes 589824 | tf_op jit(solution)/shard_map/psum | solution.py:167
  104.8 5.7 %copy-start.20 = (f32[64,64,9]{1,0,2:T(8,128)}, f32[64,64,9]{1,0,2:T(8,128)S(1)}, u32[]{:S(2)}) copy-start(f32[64,64,9]{1,0,2:T(8,128)S(1)} %fusion.104) | copy-start | bytes 442372
  104.8 6.1 %collective-permute-start.6 = (bf16[64,73,1,16]{1,0,3,2:T(8,128)(2,1)S(1)}, bf16[64,73,1,16]{1,0,3,2:T(8,128)(2,1)S(1)}, u32[]{:S(2)}, u32[]{:S(2)}) collective-permute-start(bf16[64,73,1,16]{1,0,3,2:T(8,128)(2,1)S(1)} %get-tuple-element.165), channel_id=1, source_target_pairs={{1,0},{2,1},{3,2},{5,4},{6,5},{7,6},{9,8},{10,9},{11,10},{13,12},{... | collective-permute-start | bytes 448520 | tf_op jit(solution)/shard_map/ppermute | solution.py:34
  106.1 5.3 %collective-permute-start.5 = (bf16[64,73,1,16]{1,0,3,2:T(8,128)(2,1)S(1)}, bf16[64,73,1,16]{1,0,3,2:T(8,128)(2,1)S(1)}, u32[]{:S(2)}, u32[]{:S(2)}) collective-permute-start(bf16[64,73,1,16]{1,0,3,2:T(8,128)(2,1)S(1)} %get-tuple-element.164), channel_id=1, source_target_pairs={{0,1},{1,2},{2,3},{4,5},{5,6},{6,7},{8,9},{9,10},{10,11},{12,13},{... | collective-permute-start | bytes 448520 | tf_op jit(solution)/shard_map/ppermute | solution.py:32
  (28 other events, 38.7 us)
Sparse Core Ops, SparseCore 0:
  96.0 91.5 all-reduce.7
  191.6 93.0 all-reduce.5
